TPU v7x, 32 devices: a whole 2x2x4 slice. The times are simulated.
32 devices in a mesh: scene: 4 (over y, x), row: 4 (over z), col: 2 (over core).
Axes of the slice: x: 2, y: 2, z: 4, core: 2. Of those that a mesh axis runs over, the one named last changes fastest.
Arguments:
- scenes: bfloat16 [4, 256, 128, 128], P('scene', 'row', 'col'), may hold values from -6 to 6
- cotangent: bfloat16 [4, 256, 128, 128], P('scene', 'row', 'col'), may hold values from -0.016479492 to 0.016479492
- params: float32 [294912], P(('scene', 'row', 'col')), may hold values from -0.1875 to 0.1875
- partials: float32 [32, 294912], P(('scene', 'row', 'col')), may hold values from -8 to 8
Outputs:
- sam_grad: float32 [294912], P(('scene', 'row', 'col'))
All inputs are finite; a program needn't handle non-finite values.
Results may differ from a plain program's by a relative error of at most 0.0042.
Values may be sent and summed in bfloat16 or wider, within the bound.
A program may use at most 64 MiB of HBM per device.

v0:
```python
import jax
import jax.numpy as jnp
from jax import lax
from jax.sharding import PartitionSpec as P

radius = 2.0
epsilon = 1e-06


def with_halo(cells, sides, width):
    for axis, dim in sides:
        count = lax.axis_size(axis)
        ends = count - 1
        head = lax.slice_in_dim(cells, 0, width, axis=dim)
        tail = lax.slice_in_dim(cells, cells.shape[dim] - width, cells.shape[dim], axis=dim)
        cells = jnp.concatenate(
            [
                lax.ppermute(tail, axis, [(i, (i + 1) % count) for i in range(ends)]),
                cells,
                lax.ppermute(head, axis, [((i + 1) % count, i) for i in range(ends)]),
            ],
            axis=dim,
        )
    return cells


def convolve(padded, kernel):
    return lax.conv_general_dilated(
        padded,
        kernel,
        (1, 1),
        "VALID",
        dimension_numbers=("NHWC", "HWIO", "NHWC"),
        preferred_element_type=jnp.float32,
    )


def widened(field):
    return with_halo(field, (("row", 1), ("col", 2)), 1)


def kernel_grad(padded, errors):
    height = errors.shape[1]
    width = errors.shape[2]
    rows_out = []
    for row_off in range(3):
        cols_out = []
        for col_off in range(3):
            window = padded[:, row_off : row_off + height, col_off : col_off + width, :]
            cols_out.append(
                jnp.einsum("nhwc,nhwd->cd", window, errors, preferred_element_type=jnp.float32)
            )
        rows_out.append(jnp.stack(cols_out))
    return jnp.stack(rows_out)


def on_device(scenes, cotangent, params, partials):
    local_part = partials[0]
    totals = lax.psum(local_part, ("scene", "row", "col"))
    raw_whole = lax.all_gather(params, ("scene", "row", "col"), axis=0, tiled=True)
    factor = radius / (jnp.sqrt(jnp.sum(totals * totals)) + epsilon)
    whole = (raw_whole + factor * totals).astype(jnp.bfloat16)
    channels = scenes.shape[3]
    kernels = whole.reshape(2, 3, 3, channels, channels)
    kernel_one = kernels[0]
    flipped = jnp.transpose(kernels[1][::-1, ::-1], (0, 1, 3, 2))
    padded_in = widened(scenes)
    pre = convolve(padded_in, kernel_one)
    hidden = jax.nn.silu(pre).astype(jnp.bfloat16)
    back = convolve(widened(cotangent), flipped)
    squash = jax.nn.sigmoid(pre)
    delta = (back * squash * (1.0 + pre * (1.0 - squash))).astype(jnp.bfloat16)
    grad_one = kernel_grad(padded_in, delta)
    grad_two = kernel_grad(widened(hidden), cotangent)
    local_grad = jnp.stack([grad_one, grad_two]).reshape(-1)
    return lax.psum_scatter(local_grad, ("scene", "row", "col"), scatter_dimension=0, tiled=True)


def solution(mesh):
    return jax.shard_map(
        on_device,
        mesh=mesh,
        in_specs=(
            P("scene", "row", "col", None),
            P("scene", "row", "col", None),
            P(("scene", "row", "col")),
            P(("scene", "row", "col"), None),
        ),
        out_specs=P(("scene", "row", "col")),
        check_vma=False,
    )
```

profile of v0, /device:TPU:0, one launch (start us, length us, event | category | flops | bytes accessed | tf_op | source)
XLA Modules:
  0.0 384.6 jit_solution(3427847306633833855)
XLA Ops:
  6.5 0.7 all-reduce.4.cloned.1.call-update
  7.3 0.7 all-gather.2.cloned.1.call-update
  8.1 5.1 %collective-permute-start = (bf16[1,1,64,128]{3,2,1,0:T(8,128)(2,1)S(1)}, bf16[1,1,64,128]{3,2,1,0:T(8,128)(2,1)S(1)}, u32[]{:S(2)}, u32[]{:S(2)}) collective-permute-start(bf16[1,1,64,128]{3,2,1,0:T(8,128)(2,1)S(1)} %get-tuple-element.18), channel_id=1, source_target_pairs={{0,2},{2,4},{4,6},{1,3},{3,5},{5,7},{8,10},{10,12},{12,14},{9,11},... | collective-permute-start | bytes 49160 | tf_op jit(solution)/shard_map/ppermute | solution.py:18
  13.2 1.3 collective-permute-start.1
  14.5 0.7 fusion.78
  15.2 4.5 %collective-permute-start.3 = (bf16[1,1,64,128]{3,2,1,0:T(8,128)(2,1)S(1)}, bf16[1,1,64,128]{3,2,1,0:T(8,128)(2,1)S(1)}, u32[]{:S(2)}, u32[]{:S(2)}) collective-permute-start(bf16[1,1,64,128]{3,2,1,0:T(8,128)(2,1)S(1)} %get-tuple-element.16), channel_id=1, source_target_pairs={{0,2},{2,4},{4,6},{1,3},{3,5},{5,7},{8,10},{10,12},{12,14},{9,11},... | collective-permute-start | bytes 49160 | tf_op jit(solution)/shard_map/ppermute | solution.py:18
  19.8 1.3 collective-permute-start.4
  21.1 0.6 copy-done.11
  21.8 0.6 copy-done.13
  22.5 1.3 collective-permute-start.2
  23.8 1.3 collective-permute-start.7
  25.5 2.9 collective-permute-start.5
  28.4 1.3 collective-permute-start.6
  29.7 0.6 maximum_bitcast_fusion.1
  30.8 0.8 slice.176
  31.6 0.6 maximum_bitcast_fusion
  32.7 1.0 copy-done.1
  33.7 0.8 slice.173
  34.5 112.6 %all-reduce.4.cloned.1.call-done = f32[294912]{0:T(1024)} async-done(((f32[294912]{0:T(1024)}), f32[294912]{0:T(1024)}) %all-reduce.4.cloned.1.call-update) | async-done | bytes 1179664 | tf_op jit(solution)/shard_map/psum | solution.py:59
  147.1 2.3 multiply_reduce_fusion
  150.2 53.1 %all-gather.2.cloned.1.call-done = f32[294912]{0:T(1024)} async-done(((f32[9216]{0:T(1024)}), f32[294912]{0:T(1024)}) %all-gather.2.cloned.1.call-update) | async-done | bytes 1179664 | tf_op jit(solution)/shard_map/all_gather | solution.py:60
  203.2 1.5 add_convert_fusion
  204.8 3.2 multiply_convert_fusion.1
  208.4 0.9 copy-done.2
  209.4 3.4 multiply_convert_fusion
  213.2 1.1 copy-done.4
  214.4 1.3 convolution_bitcast_fusion.13
  215.8 2.5 collective-permute-start.8
  218.4 1.6 collective-permute-start.9
  220.0 2.1 convolution_bitcast_fusion.4
  222.1 1.4 convolution_bitcast_fusion.11
  223.5 1.4 convolution_bitcast_fusion.9
  224.9 1.3 convolution_bitcast_fusion.10
  226.2 1.4 convolution_bitcast_fusion.14
  227.6 1.4 convolution_bitcast_fusion.12
  229.0 1.4 convolution_bitcast_fusion.17
  230.4 1.4 convolution_bitcast_fusion.15
  231.8 1.3 convolution_bitcast_fusion.16
  233.3 0.9 copy.53
  234.3 1.8 collective-permute-start.10
  236.1 1.3 collective-permute-start.11
  238.4 0.8 collective-permute-done.11
  239.2 0.8 maximum_maximum_fusion
  240.0 0.5 convolution_bitcast_fusion.3
  240.5 0.5 convolution_bitcast_fusion.6
  243.1 1.1 pad_maximum_fusion.1
  244.2 132.5 %all-reduce.6.cloned.1.call-done = f32[294912]{0:T(1024)} async-done(((f32[294912]{0:T(1024)}), f32[294912]{0:T(1024)}) %all-reduce.6.cloned.1.call-update) | async-done | bytes 1179664
  376.7 1.4 dynamic-slice
  (82 shorter events, 5.6 us)
Async XLA Ops:
  6.5 1.5 copy-start.3
  6.5 140.6 %all-reduce.4.cloned.1.call-start = ((), (), s32[]{:S(2)}) async-start(), calls=%async_computation.1 | async-start | bytes 2359296 | tf_op jit(solution)/shard_map/psum | solution.py:59
  7.3 196.0 %all-gather.2.cloned.1.call-start = ((), (), s32[]{:S(2)}) async-start(), calls=%async_computation | async-start | bytes 1216512 | tf_op jit(solution)/shard_map/all_gather | solution.py:60
  8.0 368.7 %all-reduce.6.cloned.1.call-start = ((), (), s32[]{:S(2)}) async-start(), calls=%async_computation.2 | async-start | bytes 2359296
  8.1 17.1 %copy-start.5 = (bf16[1,64,64,128]{3,2,1,0:T(8,128)(2,1)S(1)}, bf16[1,64,64,128]{3,2,1,0:T(8,128)(2,1)}, u32[]{:S(2)}) copy-start(bf16[1,64,64,128]{3,2,1,0:T(8,128)(2,1)} %param.5) | copy-start | bytes 3145732
  8.1 13.0 %collective-permute-start = (bf16[1,1,64,128]{3,2,1,0:T(8,128)(2,1)S(1)}, bf16[1,1,64,128]{3,2,1,0:T(8,128)(2,1)S(1)}, u32[]{:S(2)}, u32[]{:S(2)}) collective-permute-start(bf16[1,1,64,128]{3,2,1,0:T(8,128)(2,1)S(1)} %get-tuple-element.18), channel_id=1, source_target_pairs={{0,2},{2,4},{4,6},{1,3},{3,5},{5,7},{8,10},{10,12},{12,14},{9,11},... | collective-permute-start | bytes 49160 | tf_op jit(solution)/shard_map/ppermute | solution.py:18
  13.2 8.6 %collective-permute-start.1 = (bf16[1,1,64,128]{3,2,1,0:T(8,128)(2,1)S(1)}, bf16[1,1,64,128]{3,2,1,0:T(8,128)(2,1)S(1)}, u32[]{:S(2)}, u32[]{:S(2)}) collective-permute-start(bf16[1,1,64,128]{3,2,1,0:T(8,128)(2,1)S(1)} %get-tuple-element.17), channel_id=1, source_target_pairs={{2,0},{4,2},{6,4},{3,1},{5,3},{7,5},{10,8},{12,10},{14,12},{11,9},... | collective-permute-start | bytes 49160 | tf_op jit(solution)/shard_map/ppermute | solution.py:20
  15.2 9.9 %collective-permute-start.3 = (bf16[1,1,64,128]{3,2,1,0:T(8,128)(2,1)S(1)}, bf16[1,1,64,128]{3,2,1,0:T(8,128)(2,1)S(1)}, u32[]{:S(2)}, u32[]{:S(2)}) collective-permute-start(bf16[1,1,64,128]{3,2,1,0:T(8,128)(2,1)S(1)} %get-tuple-element.16), channel_id=1, source_target_pairs={{0,2},{2,4},{4,6},{1,3},{3,5},{5,7},{8,10},{10,12},{12,14},{9,11},... | collective-permute-start | bytes 49160 | tf_op jit(solution)/shard_map/ppermute | solution.py:18
  19.8 5.6 %collective-permute-start.4 = (bf16[1,1,64,128]{3,2,1,0:T(8,128)(2,1)S(1)}, bf16[1,1,64,128]{3,2,1,0:T(8,128)(2,1)S(1)}, u32[]{:S(2)}, u32[]{:S(2)}) collective-permute-start(bf16[1,1,64,128]{3,2,1,0:T(8,128)(2,1)S(1)} %get-tuple-element.15), channel_id=1, source_target_pairs={{2,0},{4,2},{6,4},{3,1},{5,3},{7,5},{10,8},{12,10},{14,12},{11,9},... | collective-permute-start | bytes 49160 | tf_op jit(solution)/shard_map/ppermute | solution.py:20
  21.1 0.6 copy-start.11
  21.8 0.6 copy-start.13
  22.5 7.2 %collective-permute-start.2 = (bf16[1,66,1,128]{3,2,1,0:T(2,128)(2,1)S(1)}, bf16[1,66,1,128]{3,2,1,0:T(2,128)(2,1)S(1)}, u32[]{:S(2)}, u32[]{:S(2)}) collective-permute-start(bf16[1,66,1,128]{3,2,1,0:T(2,128)(2,1)S(1)} %get-tuple-element.13), channel_id=1, source_target_pairs={{0,1},{2,3},{4,5},{6,7},{8,9},{10,11},{12,13},{14,15},{16,17},{18,... | collective-permute-start | bytes 50696 | tf_op jit(solution)/shard_map/ppermute | solution.py:18
  23.8 5.9 %collective-permute-start.7 = (bf16[1,66,1,128]{3,2,1,0:T(2,128)(2,1)S(1)}, bf16[1,66,1,128]{3,2,1,0:T(2,128)(2,1)S(1)}, u32[]{:S(2)}, u32[]{:S(2)}) collective-permute-start(bf16[1,66,1,128]{3,2,1,0:T(2,128)(2,1)S(1)} %get-tuple-element.14), channel_id=1, source_target_pairs={{1,0},{3,2},{5,4},{7,6},{9,8},{11,10},{13,12},{15,14},{17,16},{19,... | collective-permute-start | bytes 50696 | tf_op jit(solution)/shard_map/ppermute | solution.py:20
  25.5 6.1 %collective-permute-start.5 = (bf16[1,66,1,128]{3,2,1,0:T(2,128)(2,1)S(1)}, bf16[1,66,1,128]{3,2,1,0:T(2,128)(2,1)S(1)}, u32[]{:S(2)}, u32[]{:S(2)}) collective-permute-start(bf16[1,66,1,128]{3,2,1,0:T(2,128)(2,1)S(1)} %get-tuple-element.7), channel_id=1, source_target_pairs={{0,1},{2,3},{4,5},{6,7},{8,9},{10,11},{12,13},{14,15},{16,17},{18,... | collective-permute-start | bytes 50696 | tf_op jit(solution)/shard_map/ppermute | solution.py:18
  28.4 3.2 collective-permute-start.6
  32.7 1.0 copy-start.1
  147.1 56.1 %copy-start = (f32[294912]{0:T(1024)S(1)}, f32[294912]{0:T(1024)}, u32[]{:S(2)}) copy-start(f32[294912]{0:T(1024)} %all-reduce.4.cloned.1.call-done) | copy-start | bytes 3538948
  150.1 54.7 %copy-start.15 = (pred[8,9]{0,1:T(8,128)(4,1)S(1)}, pred[8,9]{0,1:T(8,128)(4,1)}, u32[]{:S(2)}) copy-start(pred[8,9]{0,1:T(8,128)(4,1)} %constant.21) | copy-start | bytes 220
  203.2 1.6 copy-start.9
  208.1 1.3 copy-start.2
  208.1 1.3 copy-start.10
  213.1 1.2 copy-start.4
  214.4 1.3 copy-start.7
  215.8 18.3 %collective-permute-start.8 = (bf16[1,1,64,128]{3,2,1,0:T(8,128)(2,1)S(1)}, bf16[1,1,64,128]{3,2,1,0:T(8,128)(2,1)S(1)}, u32[]{:S(2)}, u32[]{:S(2)}) collective-permute-start(bf16[1,1,64,128]{3,2,1,0:T(8,128)(2,1)S(1)} %slice.186), channel_id=1, source_target_pairs={{0,2},{2,4},{4,6},{1,3},{3,5},{5,7},{8,10},{10,12},{12,14},{9,11},... | collective-permute-start | bytes 49160 | tf_op jit(solution)/shard_map/ppermute | solution.py:18
  218.3 3.7 copy-start.8
  218.4 15.8 %collective-permute-start.9 = (bf16[1,1,64,128]{3,2,1,0:T(8,128)(2,1)S(1)}, bf16[1,1,64,128]{3,2,1,0:T(8,128)(2,1)S(1)}, u32[]{:S(2)}, u32[]{:S(2)}) collective-permute-start(bf16[1,1,64,128]{3,2,1,0:T(8,128)(2,1)S(1)} %slice.189), channel_id=1, source_target_pairs={{2,0},{4,2},{6,4},{3,1},{5,3},{7,5},{10,8},{12,10},{14,12},{11,9},... | collective-permute-start | bytes 49160 | tf_op jit(solution)/shard_map/ppermute | solution.py:20
  223.5 1.4 copy-start.14
  230.4 1.4 copy-start.12
  233.2 4.2 %copy-start.6 = (bf16[1,64,64,128]{3,2,1,0:T(8,128)(2,1)S(1)}, bf16[1,64,64,128]{3,2,1,0:T(8,128)(2,1)}, u32[]{:S(2)}) copy-start(bf16[1,64,64,128]{3,2,1,0:T(8,128)(2,1)} %param.5) | copy-start | bytes 3145732
  234.3 4.1 %collective-permute-start.10 = (bf16[1,66,1,128]{3,2,1,0:T(2,128)(2,1)S(1)}, bf16[1,66,1,128]{3,2,1,0:T(2,128)(2,1)S(1)}, u32[]{:S(2)}, u32[]{:S(2)}) collective-permute-start(bf16[1,66,1,128]{3,2,1,0:T(2,128)(2,1)S(1)} %get-tuple-element.11), channel_id=1, source_target_pairs={{0,1},{2,3},{4,5},{6,7},{8,9},{10,11},{12,13},{14,15},{16,17},{18,... | collective-permute-start | bytes 50696 | tf_op jit(solution)/shard_map/ppermute | solution.py:18
  236.1 3.1 collective-permute-start.11
Sparse Core Ops, SparseCore 0:
  12.7 134.3 all-reduce.3
  150.1 53.0 all-gather.1
  244.3 132.3 all-reduce.5
where the time goes:
time: 385 us
  waiting for transfers between devices  301 us (78%)
  starting transfers between devices  26.3 us (7%)
  matrix products  24.9 us (6%)
  between operations  14.5 us (4%)
  local copies, waits for them, and re-layouts  11.1 us (3%)
  other arithmetic  7.21 us (2%)
    unnamed x4, waiting for transfers between devices  134 us
    psum x1, waiting for transfers between devices, on_device(): totals = lax.psum(local_part, ('scene', 'row', 'col'))  113 us
    all_gather x1, waiting for transfers between devices, on_device(): lax.all_gather(params, ('scene', 'row', 'col'), axis=0, tiled=True)  53.1 us
    dot_general x18, matrix products, kernel_grad(): jnp.einsum('nhwc,nhwd->cd', window, errors, preferred_element_type=jnp.fl...  18.2 us
    ppermute x6, starting transfers between devices, with_halo(): lax.ppermute(tail, axis, [(i, (i + 1) % count) for i in range(ends)])  18.1 us
    ppermute x6, starting transfers between devices, with_halo(): lax.ppermute(head, axis, [((i + 1) % count, i) for i in range(ends)])  8.06 us
  transfers between devices with their start and end apart: 15, of which 5 were waited for; matrix products, arithmetic and copies ran while one was open for 6% of the time, Pallas kernels for 0%

commit v1 on v0

--- a/solution.py
+++ b/solution.py
@@ -56,7 +56,9 @@
 
 def on_device(scenes, cotangent, params, partials):
     local_part = partials[0]
-    totals = lax.psum(local_part, ("scene", "row", "col"))
+    totals = local_part
+    for name in ("scene", ("row", "col")):
+        totals = lax.psum(totals, name)
     raw_whole = lax.all_gather(params, ("scene", "row", "col"), axis=0, tiled=True)
     factor = radius / (jnp.sqrt(jnp.sum(totals * totals)) + epsilon)
     whole = (raw_whole + factor * totals).astype(jnp.bfloat16)

time: 385 us -> 317 us (0.82)
  waiting for transfers between devices: 301 us -> 234 us
    all_gather x1, waiting for transfers between devices: 53.1 us -> 0.03 us  [on_device(): lax.all_gather(params, ('scene', 'row', 'col'), axis=0, tiled=True)]
    psum x1 -> x2, waiting for transfers between devices: 113 us -> 98.8 us  [on_device(): totals = lax.psum(totals, name)]
    unnamed x4 -> x5, waiting for transfers between devices: 134 us -> 133 us
  transfers between devices with their start and end apart: 15 -> 16, of which waited for: 5 -> 5; matrix products, arithmetic and copies ran while one was open for 6% -> 7% of each run, Pallas kernels for 0% -> 0%
where the time goes in v1:
time: 317 us; the launch traced here: 316 us
  waiting for transfers between devices  234 us (74%)
  matrix products  24.9 us (8%)
  starting transfers between devices  24.1 us (8%)
  between operations  16.3 us (5%)
  local copies, waits for them, and re-layouts  9.82 us (3%)
  other arithmetic  7.18 us (2%)
    unnamed x5, waiting for transfers between devices  133 us
    psum x2, waiting for transfers between devices, on_device(): totals = lax.psum(totals, name)  98.8 us
    dot_general x18, matrix products, kernel_grad(): jnp.einsum('nhwc,nhwd->cd', window, errors, preferred_element_type=jnp.fl...  18.2 us
    ppermute x6, starting transfers between devices, with_halo(): lax.ppermute(tail, axis, [(i, (i + 1) % count) for i in range(ends)])  16 us
    ppermute x6, starting transfers between devices, with_halo(): lax.ppermute(head, axis, [((i + 1) % count, i) for i in range(ends)])  8.06 us
    unnamed x40, local copies, waits for them, and re-layouts  6.72 us
    conv_general_dilated x2, matrix products, convolve(): lax.conv_general_dilated(padded, kernel, (1, 1), 'VALID', dimension_numbe...  6.66 us
  transfers between devices with their start and end apart: 16, of which 5 were waited for; matrix products, arithmetic and copies ran while one was open for 7% of the time, Pallas kernels for 0%

profile of v1, /device:TPU:0, one launch (start us, length us, event | category | flops | bytes accessed | tf_op | source)
XLA Modules:
  0.0 316.0 jit_solution(9491792473995955053)
XLA Ops:
  7.4 0.7 all-reduce.5.cloned.1.call-update
  8.1 60.2 %all-reduce.5.cloned.1.call-done = f32[294912]{0:T(1024)} async-done(((f32[294912]{0:T(1024)}), f32[294912]{0:T(1024)}) %all-reduce.5.cloned.1.call-update) | async-done | bytes 1179664 | tf_op jit(solution)/shard_map/psum | solution.py:61
  68.4 0.5 all-gather.2.cloned.1.call-update
  69.0 3.4 %collective-permute-start = (bf16[1,1,64,128]{3,2,1,0:T(8,128)(2,1)S(1)}, bf16[1,1,64,128]{3,2,1,0:T(8,128)(2,1)S(1)}, u32[]{:S(2)}, u32[]{:S(2)}) collective-permute-start(bf16[1,1,64,128]{3,2,1,0:T(8,128)(2,1)S(1)} %get-tuple-element.18), channel_id=1, source_target_pairs={{0,2},{2,4},{4,6},{1,3},{3,5},{5,7},{8,10},{10,12},{12,14},{9,11},... | collective-permute-start | bytes 49160 | tf_op jit(solution)/shard_map/ppermute | solution.py:18
  72.4 1.3 collective-permute-start.1
  73.8 4.5 %collective-permute-start.3 = (bf16[1,1,64,128]{3,2,1,0:T(8,128)(2,1)S(1)}, bf16[1,1,64,128]{3,2,1,0:T(8,128)(2,1)S(1)}, u32[]{:S(2)}, u32[]{:S(2)}) collective-permute-start(bf16[1,1,64,128]{3,2,1,0:T(8,128)(2,1)S(1)} %get-tuple-element.16), channel_id=1, source_target_pairs={{0,2},{2,4},{4,6},{1,3},{3,5},{5,7},{8,10},{10,12},{12,14},{9,11},... | collective-permute-start | bytes 49160 | tf_op jit(solution)/shard_map/ppermute | solution.py:18
  78.3 1.3 collective-permute-start.4
  79.6 0.6 copy-done.11
  80.5 1.3 collective-permute-start.2
  81.8 1.3 collective-permute-start.7
  83.2 0.7 collective-permute-done.4
  84.1 2.3 collective-permute-start.5
  86.4 1.3 collective-permute-start.6
  87.7 0.6 maximum_bitcast_fusion.1
  88.8 0.8 slice.176
  89.6 0.6 maximum_bitcast_fusion
  90.7 1.0 copy-done.1
  91.7 0.8 slice.173
  92.5 38.6 %all-reduce.7.cloned.1.call-done = f32[294912]{0:T(1024)} async-done(((f32[294912]{0:T(1024)}), f32[294912]{0:T(1024)}) %all-reduce.7.cloned.1.call-update) | async-done | bytes 1179664 | tf_op jit(solution)/shard_map/psum | solution.py:61
  131.1 2.3 multiply_reduce_fusion
  134.1 1.5 add_convert_fusion
  135.7 3.2 %multiply_convert_fusion.1 = (bf16[64,8,9,128]{3,1,2,0:T(8,128)(2,1)S(1)}, f32[64,8,9,128]{3,1,2,0:T(8,128)S(1)}) fusion(pred[8,9]{0,1:T(8,128)(4,1)S(1)} %copy-done.15, bf16[3,3,128,128]{3,2,1,0:T(8,128)(2,1)S(1)} %bitcast.193, bf16[66,1,7,2,128]{4,2,3,0,1:T(8,128)(2,1)S(1)} %copy-done.9, bf16[66,1,8,9,128]{4,2,3,0,1:T(8,128)(2,1)S(1)} %copy.24), kind=kOutput, calls=%fused_computation.4 | convolution fusion | flops 1366953984 | bytes 5286984 | tf_op jit(solution)/shard_map/conv_general_dilated | solution.py:28
  139.3 0.9 copy-done.2
  140.3 3.4 %multiply_convert_fusion = bf16[64,8,9,128]{3,1,2,0:T(8,128)(2,1)S(1)} fusion(f32[64,8,9,128]{3,1,2,0:T(8,128)S(1)} %get-tuple-element.22, bf16[3,3,128,128]{3,2,1,0:T(8,128)(2,1)S(1)} %bitcast.192, bf16[66,1,7,2,128]{4,2,3,0,1:T(8,128)(2,1)S(1)} %copy-done.10, bf16[66,1,8,9,128]{4,2,3,0,1:T(8,128)(2,1)S(1)} %copy-done.2, pred[8,9]{0,1:T(8,128)(4,1)S(1)} %copy-done.15), kind=kOutput, calls=%fused_computation.3 | convolution fusion | flops 1369903104 | bytes 5286984 | tf_op jit(solution)/shard_map/conv_general_dilated | solution.py:28
  144.1 1.1 copy-done.4
  145.3 1.3 convolution_bitcast_fusion.13
  146.7 3.1 collective-permute-start.8
  149.9 1.6 collective-permute-start.9
  151.5 2.1 convolution_bitcast_fusion.4
  153.7 1.4 convolution_bitcast_fusion.11
  155.0 1.4 convolution_bitcast_fusion.9
  156.5 1.3 convolution_bitcast_fusion.10
  157.8 1.4 convolution_bitcast_fusion.14
  159.2 1.4 convolution_bitcast_fusion.12
  160.6 1.4 convolution_bitcast_fusion.17
  162.0 1.4 convolution_bitcast_fusion.15
  163.4 1.3 convolution_bitcast_fusion.16
  164.8 0.9 copy.53
  165.8 1.3 collective-permute-start.10
  167.1 1.3 collective-permute-start.11
  169.4 0.8 collective-permute-done.11
  170.2 0.8 maximum_maximum_fusion
  171.1 0.5 convolution_bitcast_fusion.3
  171.6 0.5 convolution_bitcast_fusion.6
  173.0 0.5 convolution_bitcast_fusion
  174.1 1.1 pad_maximum_fusion.1
  175.2 132.0 %all-reduce.9.cloned.1.call-done = f32[294912]{0:T(1024)} async-done(((f32[294912]{0:T(1024)}), f32[294912]{0:T(1024)}) %all-reduce.9.cloned.1.call-update) | async-done | bytes 1179664
  307.2 1.4 dynamic-slice
  (85 shorter events, 5.1 us)
Async XLA Ops:
  7.4 61.7 %copy-start.3 = (bf16[1,64,64,128]{3,2,1,0:T(8,128)(2,1)S(1)}, bf16[1,64,64,128]{3,2,1,0:T(8,128)(2,1)}, u32[]{:S(2)}) copy-start(bf16[1,64,64,128]{3,2,1,0:T(8,128)(2,1)} %param.4) | copy-start | bytes 3145732
  7.4 61.0 %all-reduce.5.cloned.1.call-start = ((), (), s32[]{:S(2)}) async-start(), calls=%async_computation.1 | async-start | bytes 2359296 | tf_op jit(solution)/shard_map/psum | solution.py:61
  7.4 66.4 %copy-start.5 = (bf16[1,64,64,128]{3,2,1,0:T(8,128)(2,1)S(1)}, bf16[1,64,64,128]{3,2,1,0:T(8,128)(2,1)}, u32[]{:S(2)}) copy-start(bf16[1,64,64,128]{3,2,1,0:T(8,128)(2,1)} %param.5) | copy-start | bytes 3145732
  8.1 123.1 %all-reduce.7.cloned.1.call-start = ((), (), s32[]{:S(2)}) async-start(), calls=%async_computation.2 | async-start | bytes 2359296 | tf_op jit(solution)/shard_map/psum | solution.py:61
  68.4 65.7 %all-gather.2.cloned.1.call-start = ((), (), s32[]{:S(2)}) async-start(), calls=%async_computation | async-start | bytes 1216512 | tf_op jit(solution)/shard_map/all_gather | solution.py:62
  69.0 238.2 %all-reduce.9.cloned.1.call-start = ((), (), s32[]{:S(2)}) async-start(), calls=%async_computation.3 | async-start | bytes 2359296
  69.0 10.6 %collective-permute-start = (bf16[1,1,64,128]{3,2,1,0:T(8,128)(2,1)S(1)}, bf16[1,1,64,128]{3,2,1,0:T(8,128)(2,1)S(1)}, u32[]{:S(2)}, u32[]{:S(2)}) collective-permute-start(bf16[1,1,64,128]{3,2,1,0:T(8,128)(2,1)S(1)} %get-tuple-element.18), channel_id=1, source_target_pairs={{0,2},{2,4},{4,6},{1,3},{3,5},{5,7},{8,10},{10,12},{12,14},{9,11},... | collective-permute-start | bytes 49160 | tf_op jit(solution)/shard_map/ppermute | solution.py:18
  72.4 7.9 %collective-permute-start.1 = (bf16[1,1,64,128]{3,2,1,0:T(8,128)(2,1)S(1)}, bf16[1,1,64,128]{3,2,1,0:T(8,128)(2,1)S(1)}, u32[]{:S(2)}, u32[]{:S(2)}) collective-permute-start(bf16[1,1,64,128]{3,2,1,0:T(8,128)(2,1)S(1)} %get-tuple-element.17), channel_id=1, source_target_pairs={{2,0},{4,2},{6,4},{3,1},{5,3},{7,5},{10,8},{12,10},{14,12},{11,9},... | collective-permute-start | bytes 49160 | tf_op jit(solution)/shard_map/ppermute | solution.py:20
  73.8 9.3 %collective-permute-start.3 = (bf16[1,1,64,128]{3,2,1,0:T(8,128)(2,1)S(1)}, bf16[1,1,64,128]{3,2,1,0:T(8,128)(2,1)S(1)}, u32[]{:S(2)}, u32[]{:S(2)}) collective-permute-start(bf16[1,1,64,128]{3,2,1,0:T(8,128)(2,1)S(1)} %get-tuple-element.16), channel_id=1, source_target_pairs={{0,2},{2,4},{4,6},{1,3},{3,5},{5,7},{8,10},{10,12},{12,14},{9,11},... | collective-permute-start | bytes 49160 | tf_op jit(solution)/shard_map/ppermute | solution.py:18
  78.3 5.7 %collective-permute-start.4 = (bf16[1,1,64,128]{3,2,1,0:T(8,128)(2,1)S(1)}, bf16[1,1,64,128]{3,2,1,0:T(8,128)(2,1)S(1)}, u32[]{:S(2)}, u32[]{:S(2)}) collective-permute-start(bf16[1,1,64,128]{3,2,1,0:T(8,128)(2,1)S(1)} %get-tuple-element.15), channel_id=1, source_target_pairs={{2,0},{4,2},{6,4},{3,1},{5,3},{7,5},{10,8},{12,10},{14,12},{11,9},... | collective-permute-start | bytes 49160 | tf_op jit(solution)/shard_map/ppermute | solution.py:20
  79.6 0.6 copy-start.11
  80.4 3.7 %copy-start.13 = (bf16[1,1,64,128]{3,2,1,0:T(8,128)(2,1)}, bf16[1,1,64,128]{3,2,1,0:T(8,128)(2,1)S(1)}, u32[]{:S(2)}) copy-start(bf16[1,1,64,128]{3,2,1,0:T(8,128)(2,1)S(1)} %collective-permute-done.1) | copy-start | bytes 49156
  80.5 7.2 %collective-permute-start.2 = (bf16[1,66,1,128]{3,2,1,0:T(2,128)(2,1)S(1)}, bf16[1,66,1,128]{3,2,1,0:T(2,128)(2,1)S(1)}, u32[]{:S(2)}, u32[]{:S(2)}) collective-permute-start(bf16[1,66,1,128]{3,2,1,0:T(2,128)(2,1)S(1)} %get-tuple-element.13), channel_id=1, source_target_pairs={{0,1},{2,3},{4,5},{6,7},{8,9},{10,11},{12,13},{14,15},{16,17},{18,... | collective-permute-start | bytes 50696 | tf_op jit(solution)/shard_map/ppermute | solution.py:18
  81.8 5.9 %collective-permute-start.7 = (bf16[1,66,1,128]{3,2,1,0:T(2,128)(2,1)S(1)}, bf16[1,66,1,128]{3,2,1,0:T(2,128)(2,1)S(1)}, u32[]{:S(2)}, u32[]{:S(2)}) collective-permute-start(bf16[1,66,1,128]{3,2,1,0:T(2,128)(2,1)S(1)} %get-tuple-element.14), channel_id=1, source_target_pairs={{1,0},{3,2},{5,4},{7,6},{9,8},{11,10},{13,12},{15,14},{17,16},{19,... | collective-permute-start | bytes 50696 | tf_op jit(solution)/shard_map/ppermute | solution.py:20
  84.1 5.5 %collective-permute-start.5 = (bf16[1,66,1,128]{3,2,1,0:T(2,128)(2,1)S(1)}, bf16[1,66,1,128]{3,2,1,0:T(2,128)(2,1)S(1)}, u32[]{:S(2)}, u32[]{:S(2)}) collective-permute-start(bf16[1,66,1,128]{3,2,1,0:T(2,128)(2,1)S(1)} %get-tuple-element.7), channel_id=1, source_target_pairs={{0,1},{2,3},{4,5},{6,7},{8,9},{10,11},{12,13},{14,15},{16,17},{18,... | collective-permute-start | bytes 50696 | tf_op jit(solution)/shard_map/ppermute | solution.py:18
  86.4 3.2 %collective-permute-start.6 = (bf16[1,66,1,128]{3,2,1,0:T(2,128)(2,1)S(1)}, bf16[1,66,1,128]{3,2,1,0:T(2,128)(2,1)S(1)}, u32[]{:S(2)}, u32[]{:S(2)}) collective-permute-start(bf16[1,66,1,128]{3,2,1,0:T(2,128)(2,1)S(1)} %get-tuple-element.8), channel_id=1, source_target_pairs={{1,0},{3,2},{5,4},{7,6},{9,8},{11,10},{13,12},{15,14},{17,16},{19,... | collective-permute-start | bytes 50696 | tf_op jit(solution)/shard_map/ppermute | solution.py:20
  90.7 1.0 copy-start.1
  131.1 3.0 copy-start
  134.1 1.6 copy-start.15
  134.1 1.6 copy-start.9
  139.0 1.3 copy-start.2
  139.0 1.3 copy-start.10
  144.0 1.2 copy-start.4
  145.3 1.3 copy-start.7
  146.7 19.0 %collective-permute-start.8 = (bf16[1,1,64,128]{3,2,1,0:T(8,128)(2,1)S(1)}, bf16[1,1,64,128]{3,2,1,0:T(8,128)(2,1)S(1)}, u32[]{:S(2)}, u32[]{:S(2)}) collective-permute-start(bf16[1,1,64,128]{3,2,1,0:T(8,128)(2,1)S(1)} %slice.186), channel_id=1, source_target_pairs={{0,2},{2,4},{4,6},{1,3},{3,5},{5,7},{8,10},{10,12},{12,14},{9,11},... | collective-permute-start | bytes 49160 | tf_op jit(solution)/shard_map/ppermute | solution.py:18
  149.9 3.7 %copy-start.8 = (bf16[64,1,64,128]{3,0,2,1:T(8,128)(2,1)S(1)}, bf16[64,1,64,128]{3,0,2,1:T(8,128)(2,1)}, u32[]{:S(2)}) copy-start(bf16[64,1,64,128]{3,0,2,1:T(8,128)(2,1)} %copy-done.7) | copy-start | bytes 3145732
  149.9 15.8 %collective-permute-start.9 = (bf16[1,1,64,128]{3,2,1,0:T(8,128)(2,1)S(1)}, bf16[1,1,64,128]{3,2,1,0:T(8,128)(2,1)S(1)}, u32[]{:S(2)}, u32[]{:S(2)}) collective-permute-start(bf16[1,1,64,128]{3,2,1,0:T(8,128)(2,1)S(1)} %slice.189), channel_id=1, source_target_pairs={{2,0},{4,2},{6,4},{3,1},{5,3},{7,5},{10,8},{12,10},{14,12},{11,9},... | collective-permute-start | bytes 49160 | tf_op jit(solution)/shard_map/ppermute | solution.py:20
  155.0 1.4 copy-start.14
  162.0 1.4 copy-start.12
  164.8 3.6 %copy-start.6 = (bf16[1,64,64,128]{3,2,1,0:T(8,128)(2,1)S(1)}, bf16[1,64,64,128]{3,2,1,0:T(8,128)(2,1)}, u32[]{:S(2)}) copy-start(bf16[1,64,64,128]{3,2,1,0:T(8,128)(2,1)} %param.5) | copy-start | bytes 3145732
  165.8 3.6 %collective-permute-start.10 = (bf16[1,66,1,128]{3,2,1,0:T(2,128)(2,1)S(1)}, bf16[1,66,1,128]{3,2,1,0:T(2,128)(2,1)S(1)}, u32[]{:S(2)}, u32[]{:S(2)}) collective-permute-start(bf16[1,66,1,128]{3,2,1,0:T(2,128)(2,1)S(1)} %get-tuple-element.11), channel_id=1, source_target_pairs={{0,1},{2,3},{4,5},{6,7},{8,9},{10,11},{12,13},{14,15},{16,17},{18,... | collective-permute-start | bytes 50696 | tf_op jit(solution)/shard_map/ppermute | solution.py:18
  167.1 3.1 collective-permute-start.11
Sparse Core Ops, SparseCore 0:
  11.3 57.0 all-reduce.4
  70.7 60.3 all-reduce.6
Sparse Core Ops, SparseCore 1:
  71.9 55.4 all-gather.1
  175.3 131.8 all-reduce.8
